TPU v7x, 256 devices: a whole 4x4x8 slice. The times are simulated.
256 devices in a mesh: rows: 8 (over x, core), cols: 32 (over y, z).
Axes of the slice: x: 4, y: 4, z: 8, core: 2. Of those that a mesh axis runs over, the one named last changes fastest.
Arguments:
- features: bfloat16 [256, 4096, 1536], P('rows', 'cols'), may hold values from -6 to 6
- projection: bfloat16 [1536, 128], replicated, may hold values from -0.4375 to 0.4375
- prev_dist: float32 [256, 4096], P('rows', 'cols'), may hold values from 0.5 to 3
- valid: int32 [256, 4096], P('rows', 'cols'), may hold values 0 or 1
- pick_owner: int32 [512], replicated, may hold values from 0 to 255, as said below
- pick_slot: int32 [512], replicated, may hold values from 0 to 4095, as said below
Outputs:
- min_dist: float32 [256, 4096], P('rows', 'cols')
Inputs may be any that keep to these rules, and one draw needn't show every extreme that they name: `pick_owner`: no two picks name the same patch; picks fall on devices at random. `pick_slot`: see pick_owner.
All inputs are finite; a program needn't handle non-finite values. No bound on the sum of `valid` on one device may be relied on, other than what follows from the above.
Results may differ from a plain program's by a relative error of at most 0.0003.
Values may be sent and summed in bfloat16 or wider, within the bound.
A program may use at most 128 MiB of HBM per device.

v0:
```python
import jax
import jax.numpy as jnp
from jax import lax
from jax.sharding import PartitionSpec as P

D_PROJ = 128


def padded_2(block, sides, width):
    for axis, dim in sides:
        count = lax.axis_size(axis)
        forward = [(i, i + 1) for i in range(count - 1)]
        backward = [(target, source) for source, target in forward]
        low = lax.ppermute(
            lax.slice_in_dim(block, block.shape[dim] - width, None, axis=dim), axis, forward
        )
        high = lax.ppermute(lax.slice_in_dim(block, 0, width, axis=dim), axis, backward)
        block = jnp.concatenate([low, block, high], axis=dim)
    return block


def window_sum(padded, rows_dev, cols_dev):
    total = jnp.zeros((rows_dev, cols_dev, padded.shape[2]), jnp.float32)
    for row_off in range(3):
        for col_off in range(3):
            total = total + padded[
                row_off : row_off + rows_dev, col_off : col_off + cols_dev
            ].astype(jnp.float32)
    return total / 9.0


def shards(features, projection, prev_dist, valid, pick_owner, pick_slot):
    rows_dev, cols_dev, channels = features.shape
    proj_full = projection.astype(jnp.float32)
    own_index = lax.axis_index("rows") * lax.axis_size("cols") + lax.axis_index("cols")
    owned = pick_owner == own_index
    padded = padded_2(features, (("rows", 0), ("cols", 1)), 1)
    pooled = window_sum(padded, rows_dev, cols_dev).reshape(rows_dev * cols_dev, channels)
    projected = jnp.dot(pooled, proj_full, precision=lax.Precision.HIGHEST)
    local_rows = jnp.where(owned[:, None], projected[pick_slot], jnp.float32(0.0))
    pick_rows = lax.psum(local_rows, ("rows", "cols"))
    pick_sq = jnp.sum(pick_rows * pick_rows, axis=1)
    own_sq = jnp.sum(projected * projected, axis=1)
    inner_prod = jnp.dot(projected, pick_rows.T, precision=lax.Precision.HIGHEST)
    scaled_gap = (own_sq[:, None] + pick_sq[None, :] - 2.0 * inner_prod) / D_PROJ
    nearest = jnp.min(scaled_gap, axis=1).reshape(rows_dev, cols_dev)
    return jnp.where(valid == 1, jnp.minimum(prev_dist, nearest), jnp.float32(0.0))


def solution(mesh):
    return jax.shard_map(
        shards,
        mesh=mesh,
        in_specs=(P("rows", "cols", None), P(), P("rows", "cols"), P("rows", "cols"), P(), P()),
        out_specs=P("rows", "cols"),
        check_vma=False,
    )
```

profile of v0, /device:TPU:2, one launch (start us, length us, event | category | flops | bytes accessed | tf_op | source)
XLA Modules:
  0.0 382.1 jit_solution(17740806826330092399)
XLA Ops:
  6.5 0.0 copy-start
  6.5 0.0 all-reduce.2.cloned.1.call-start
  6.5 1.2 fusion.6
  7.8 1.9 collective-permute-start
  9.7 3.6 collective-permute-start.1
  13.3 0.7 broadcast_compare_fusion
  14.0 0.7 compare_select_fusion
  14.7 2.1 collective-permute-done
  16.9 6.7 %constant_dynamic-update-slice_fusion.1 = bf16[34,128,1536]{2,1,0:T(8,128)(2,1)S(1)} fusion(bf16[34,128,1536]{2,1,0:T(8,128)(2,1)S(1)} %constant_dynamic-update-slice_fusion.2, bf16[32,128,1536]{2,1,0:T(8,128)(2,1)} %param.6), kind=kLoop, calls=%fused_computation.25 | loop fusion | bytes 25165824
  23.6 0.0 collective-permute-done.1
  23.6 0.0 copy-start.1
  23.6 4.8 %copy-done.1 = bf16[34,128,1536]{2,1,0:T(8,128)(2,1)} copy-done((bf16[34,128,1536]{2,1,0:T(8,128)(2,1)}, bf16[34,128,1536]{2,1,0:T(8,128)(2,1)S(1)}, u32[]{:S(2)}) %copy-start.1) | copy-done | bytes 13369368
  28.5 0.3 fusion.5
  28.8 3.8 %collective-permute-start.2 = (bf16[34,1,1536]{2,0,1:T(8,128)(2,1)S(1)}, bf16[34,1,1536]{2,0,1:T(8,128)(2,1)S(1)}, u32[]{:S(2)}, u32[]{:S(2)}) collective-permute-start(bf16[34,1,1536]{2,0,1:T(8,128)(2,1)S(1)} %copy.15), channel_id=1, source_target_pairs={{0,1},{1,2},{2,3},{3,4},{4,5},{5,6},{6,7},{7,8},{8,9},{9,10},{10,1... | collective-permute-start | bytes 313352 | tf_op jit(solution)/shard_map/ppermute | solution.py:14
  32.7 1.3 collective-permute-start.3
  34.0 1.1 collective-permute-done.2
  35.1 0.2 copy.16
  35.2 4.2 %collective-permute-done.3 = bf16[34,1,1536]{2,0,1:T(8,128)(2,1)S(1)} collective-permute-done((bf16[34,1,1536]{2,0,1:T(8,128)(2,1)S(1)}, bf16[34,1,1536]{2,0,1:T(8,128)(2,1)S(1)}, u32[]{:S(2)}, u32[]{:S(2)}) %collective-permute-start.3) | collective-permute-done | bytes 104480 | tf_op jit(solution)/shard_map/ppermute | solution.py:17
  39.5 0.2 copy.18
  39.6 47.2 %add_multiply_fusion = f32[32,128,1536]{2,1,0:T(8,128)} fusion(bf16[32,128,1536]{2,1,0:T(8,128)(2,1)} %param.6, bf16[34,128,1536]{2,1,0:T(8,128)(2,1)} %copy-done.1, bf16[34,1,1536]{2,1,0:T(2,128)(2,1)S(1)} %copy.18, bf16[34,1,1536]{2,1,0:T(2,128)(2,1)S(1)} %copy.16, bf16[1,128,1536]{2,1,0:T(8,128)(2,1)S(1)} %collective-permute-done.1, ...), kind=kLoop, calls=%fused_computation.1 | loop fusion | flops 264241152 | bytes 52113408 | tf_op jit(solution)/shard_map/div | solution.py:29
  86.8 0.0 copy-done
  86.9 18.7 %multiply_reduce_fusion.1 = (f32[4096]{0:T(1024)S(1)}, f32[4096,128]{0,1:T(8,128)S(1)}) fusion(f32[4096,1536]{1,0:T(8,128)} %bitcast.9, bf16[1536,128]{1,0:T(8,128)(2,1)S(1)} %copy-done), kind=kOutput, calls=%fused_computation.19 | convolution fusion | flops 9664720896 | bytes 27672576 | tf_op jit(solution)/shard_map/dot_general | solution.py:39
  105.6 0.0 copy-start.2
  105.6 0.0 copy-start.3
  105.6 1.9 copy.19
  107.5 2.6 gather_fusion
  110.1 0.8 broadcast_select_fusion
  111.0 0.0 all-reduce.2.cloned.1.call-update
  111.0 253.3 %all-reduce.2.cloned.1.call-done = f32[512,128]{1,0:T(8,128)} async-done(((f32[512,128]{1,0:T(8,128)}), f32[512,128]{1,0:T(8,128)}) %all-reduce.2.cloned.1.call-update) | async-done | bytes 262160 | tf_op jit(solution)/shard_map/psum | solution.py:41
  364.3 1.1 multiply_reduce_fusion.2
  365.4 9.2 %multiply_reduce_fusion = f32[4096]{0:T(1024)S(1)} fusion(f32[4096,128]{0,1:T(8,128)S(1)} %get-tuple-element.10, f32[512,128]{1,0:T(8,128)} %all-reduce.2.cloned.1.call-done, f32[512]{0:T(512)S(1)} %multiply_reduce_fusion.2, f32[4096]{0:T(1024)S(1)} %get-tuple-element.9), kind=kOutput, calls=%fused_computation.18 | convolution fusion | flops 3231707136 | bytes 2394112 | tf_op jit(solution)/shard_map/dot_general | solution.py:44
  374.6 0.0 copy-done.2
  374.6 0.0 copy-done.3
  374.7 0.6 fusion.4
  (5 shorter events, 0.1 us)
Async XLA Ops:
  6.5 80.3 %copy-start = (bf16[1536,128]{1,0:T(8,128)(2,1)S(1)}, bf16[1536,128]{1,0:T(8,128)(2,1)}, u32[]{:S(2)}) copy-start(bf16[1536,128]{1,0:T(8,128)(2,1)} %param.7) | copy-start | bytes 1179652
  6.5 357.8 %all-reduce.2.cloned.1.call-start = ((), (), s32[]{:S(2)}) async-start(), calls=%async_computation | async-start | bytes 524288 | tf_op jit(solution)/shard_map/psum | solution.py:41
  7.8 9.1 %collective-permute-start = (bf16[1,128,1536]{2,1,0:T(8,128)(2,1)S(1)}, bf16[1,128,1536]{2,1,0:T(8,128)(2,1)S(1)}, u32[]{:S(2)}, u32[]{:S(2)}) collective-permute-start(bf16[1,128,1536]{2,1,0:T(8,128)(2,1)S(1)} %get-tuple-element.8), channel_id=1, source_target_pairs={{0,32},{32,64},{64,96},{96,128},{128,160},{160,192},{192,224},{1,3... | collective-permute-start | bytes 1179656 | tf_op jit(solution)/shard_map/ppermute | solution.py:14
  9.7 13.9 %collective-permute-start.1 = (bf16[1,128,1536]{2,1,0:T(8,128)(2,1)S(1)}, bf16[1,128,1536]{2,1,0:T(8,128)(2,1)S(1)}, u32[]{:S(2)}, u32[]{:S(2)}) collective-permute-start(bf16[1,128,1536]{2,1,0:T(8,128)(2,1)S(1)} %get-tuple-element.7), channel_id=1, source_target_pairs={{32,0},{64,32},{96,64},{128,96},{160,128},{192,160},{224,192},{33,... | collective-permute-start | bytes 1179656 | tf_op jit(solution)/shard_map/ppermute | solution.py:17
  23.6 4.8 %copy-start.1 = (bf16[34,128,1536]{2,1,0:T(8,128)(2,1)}, bf16[34,128,1536]{2,1,0:T(8,128)(2,1)S(1)}, u32[]{:S(2)}) copy-start(bf16[34,128,1536]{2,1,0:T(8,128)(2,1)S(1)} %constant_dynamic-update-slice_fusion) | copy-start | bytes 40108036
  28.8 6.3 %collective-permute-start.2 = (bf16[34,1,1536]{2,0,1:T(8,128)(2,1)S(1)}, bf16[34,1,1536]{2,0,1:T(8,128)(2,1)S(1)}, u32[]{:S(2)}, u32[]{:S(2)}) collective-permute-start(bf16[34,1,1536]{2,0,1:T(8,128)(2,1)S(1)} %copy.15), channel_id=1, source_target_pairs={{0,1},{1,2},{2,3},{3,4},{4,5},{5,6},{6,7},{7,8},{8,9},{9,10},{10,1... | collective-permute-start | bytes 313352 | tf_op jit(solution)/shard_map/ppermute | solution.py:14
  32.7 6.8 %collective-permute-start.3 = (bf16[34,1,1536]{2,0,1:T(8,128)(2,1)S(1)}, bf16[34,1,1536]{2,0,1:T(8,128)(2,1)S(1)}, u32[]{:S(2)}, u32[]{:S(2)}) collective-permute-start(bf16[34,1,1536]{2,0,1:T(8,128)(2,1)S(1)} %copy.17), channel_id=1, source_target_pairs={{1,0},{2,1},{3,2},{4,3},{5,4},{6,5},{7,6},{8,7},{9,8},{10,9},{11,1... | collective-permute-start | bytes 313352 | tf_op jit(solution)/shard_map/ppermute | solution.py:17
  105.6 269.0 %copy-start.2 = (f32[32,128]{1,0:T(8,128)S(1)}, f32[32,128]{1,0:T(8,128)}, u32[]{:S(2)}) copy-start(f32[32,128]{1,0:T(8,128)} %param.8) | copy-start | bytes 49156
  105.6 269.0 %copy-start.3 = (s32[32,128]{1,0:T(8,128)S(1)}, s32[32,128]{1,0:T(8,128)}, u32[]{:S(2)}) copy-start(s32[32,128]{1,0:T(8,128)} %param.9) | copy-start | bytes 49156
Sparse Core Ops, SparseCore 0:
  111.1 253.1 all-reduce.1
where the time goes:
time: 382 us
  waiting for transfers between devices  261 us (68%)
  other arithmetic  51.2 us (13%)
  matrix products  27.9 us (7%)
  local copies, waits for them, and re-layouts  18 us (5%)
  between operations  13.6 us (4%)
  starting transfers between devices  10.7 us (3%)
    psum x1, waiting for transfers between devices, shards(): pick_rows = lax.psum(local_rows, ('rows', 'cols'))  253 us
    div x1, other arithmetic, window_sum(): return total / 9.0  47.2 us
    dot_general x1, matrix products, shards(): projected = jnp.dot(pooled, proj_full, precision=lax.Precision.HIGHEST)  18.7 us
    unnamed x10, local copies, waits for them, and re-layouts  11.6 us
    dot_general x1, matrix products, shards(): jnp.dot(projected, pick_rows.T, precision=lax.Precision.HIGHEST)  9.21 us
  transfers between devices with their start and end apart: 5, of which 4 were waited for; matrix products, arithmetic and copies ran while one was open for 2% of the time, Pallas kernels for 0%

commit v1 on v0

--- a/solution.py
+++ b/solution.py
@@ -38,7 +38,9 @@
     pooled = window_sum(padded, rows_dev, cols_dev).reshape(rows_dev * cols_dev, channels)
     projected = jnp.dot(pooled, proj_full, precision=lax.Precision.HIGHEST)
     local_rows = jnp.where(owned[:, None], projected[pick_slot], jnp.float32(0.0))
-    pick_rows = lax.psum(local_rows, ("rows", "cols"))
+    pick_rows = local_rows
+    for over in ("rows", "cols"):
+        pick_rows = lax.psum(pick_rows, over)
     pick_sq = jnp.sum(pick_rows * pick_rows, axis=1)
     own_sq = jnp.sum(projected * projected, axis=1)
     inner_prod = jnp.dot(projected, pick_rows.T, precision=lax.Precision.HIGHEST)

time: 382 us -> 344 us (0.901)
  waiting for transfers between devices: 261 us -> 222 us
    psum x1 -> x2, waiting for transfers between devices: 253 us -> 215 us  [shards(): pick_rows = lax.psum(pick_rows, over)]
  transfers between devices with their start and end apart: 5 -> 6, of which waited for: 4 -> 5; matrix products, arithmetic and copies ran while one was open for 2% -> 2% of each run, Pallas kernels for 0% -> 0%
where the time goes in v1:
time: 344 us
  waiting for transfers between devices  222 us (65%)
  other arithmetic  51.2 us (15%)
  matrix products  27.8 us (8%)
  local copies, waits for them, and re-layouts  18 us (5%)
  between operations  13.6 us (4%)
  starting transfers between devices  10.9 us (3%)
    psum x2, waiting for transfers between devices, shards(): pick_rows = lax.psum(pick_rows, over)  215 us
    div x1, other arithmetic, window_sum(): return total / 9.0  47.2 us
    dot_general x1, matrix products, shards(): projected = jnp.dot(pooled, proj_full, precision=lax.Precision.HIGHEST)  18.7 us
    unnamed x10, local copies, waits for them, and re-layouts  11.6 us
    dot_general x1, matrix products, shards(): jnp.dot(projected, pick_rows.T, precision=lax.Precision.HIGHEST)  9.02 us
  transfers between devices with their start and end apart: 6, of which 5 were waited for; matrix products, arithmetic and copies ran while one was open for 2% of the time, Pallas kernels for 0%

profile of v1, /device:TPU:2, one launch (start us, length us, event | category | flops | bytes accessed | tf_op | source)
XLA Modules:
  0.0 343.7 jit_solution(8365192781819268430)
XLA Ops:
  6.5 0.0 copy-start
  6.5 0.0 all-reduce.3.cloned.1.call-start
  6.5 1.2 fusion.6
  7.8 1.9 collective-permute-start
  9.7 3.6 %collective-permute-start.1 = (bf16[1,128,1536]{2,1,0:T(8,128)(2,1)S(1)}, bf16[1,128,1536]{2,1,0:T(8,128)(2,1)S(1)}, u32[]{:S(2)}, u32[]{:S(2)}) collective-permute-start(bf16[1,128,1536]{2,1,0:T(8,128)(2,1)S(1)} %get-tuple-element.7), channel_id=1, source_target_pairs={{32,0},{64,32},{96,64},{128,96},{160,128},{192,160},{224,192},{33,... | collective-permute-start | bytes 1179656 | tf_op jit(solution)/shard_map/ppermute | solution.py:17
  13.3 0.7 broadcast_compare_fusion
  14.0 0.7 compare_select_fusion
  14.7 2.1 collective-permute-done
  16.9 6.7 %constant_dynamic-update-slice_fusion.1 = bf16[34,128,1536]{2,1,0:T(8,128)(2,1)S(1)} fusion(bf16[34,128,1536]{2,1,0:T(8,128)(2,1)S(1)} %constant_dynamic-update-slice_fusion.2, bf16[32,128,1536]{2,1,0:T(8,128)(2,1)} %param.6), kind=kLoop, calls=%fused_computation.25 | loop fusion | bytes 25165824
  23.6 0.0 collective-permute-done.1
  23.6 0.0 copy-start.1
  23.6 4.8 %copy-done.1 = bf16[34,128,1536]{2,1,0:T(8,128)(2,1)} copy-done((bf16[34,128,1536]{2,1,0:T(8,128)(2,1)}, bf16[34,128,1536]{2,1,0:T(8,128)(2,1)S(1)}, u32[]{:S(2)}) %copy-start.1) | copy-done | bytes 13369368
  28.5 0.3 fusion.5
  28.8 3.8 %collective-permute-start.2 = (bf16[34,1,1536]{2,0,1:T(8,128)(2,1)S(1)}, bf16[34,1,1536]{2,0,1:T(8,128)(2,1)S(1)}, u32[]{:S(2)}, u32[]{:S(2)}) collective-permute-start(bf16[34,1,1536]{2,0,1:T(8,128)(2,1)S(1)} %copy.15), channel_id=1, source_target_pairs={{0,1},{1,2},{2,3},{3,4},{4,5},{5,6},{6,7},{7,8},{8,9},{9,10},{10,1... | collective-permute-start | bytes 313352 | tf_op jit(solution)/shard_map/ppermute | solution.py:14
  32.7 1.3 collective-permute-start.3
  34.0 1.1 collective-permute-done.2
  35.1 0.2 copy.16
  35.2 4.2 %collective-permute-done.3 = bf16[34,1,1536]{2,0,1:T(8,128)(2,1)S(1)} collective-permute-done((bf16[34,1,1536]{2,0,1:T(8,128)(2,1)S(1)}, bf16[34,1,1536]{2,0,1:T(8,128)(2,1)S(1)}, u32[]{:S(2)}, u32[]{:S(2)}) %collective-permute-start.3) | collective-permute-done | bytes 104480 | tf_op jit(solution)/shard_map/ppermute | solution.py:17
  39.5 0.2 copy.18
  39.6 47.2 %add_multiply_fusion = f32[32,128,1536]{2,1,0:T(8,128)} fusion(bf16[32,128,1536]{2,1,0:T(8,128)(2,1)} %param.6, bf16[34,128,1536]{2,1,0:T(8,128)(2,1)} %copy-done.1, bf16[34,1,1536]{2,1,0:T(2,128)(2,1)S(1)} %copy.18, bf16[34,1,1536]{2,1,0:T(2,128)(2,1)S(1)} %copy.16, bf16[1,128,1536]{2,1,0:T(8,128)(2,1)S(1)} %collective-permute-done.1, ...), kind=kLoop, calls=%fused_computation.1 | loop fusion | flops 264241152 | bytes 52113408 | tf_op jit(solution)/shard_map/div | solution.py:29
  86.9 0.0 copy-done
  86.9 18.7 %multiply_reduce_fusion.1 = (f32[4096]{0:T(1024)S(1)}, f32[4096,128]{0,1:T(8,128)S(1)}) fusion(f32[4096,1536]{1,0:T(8,128)} %bitcast.9, bf16[1536,128]{1,0:T(8,128)(2,1)S(1)} %copy-done), kind=kOutput, calls=%fused_computation.19 | convolution fusion | flops 9664720896 | bytes 27672576 | tf_op jit(solution)/shard_map/dot_general | solution.py:39
  105.6 0.0 copy-start.2
  105.6 0.0 copy-start.3
  105.6 1.9 copy.19
  107.5 2.6 gather_fusion
  110.1 0.8 broadcast_select_fusion
  111.0 0.0 all-reduce.3.cloned.1.call-update
  111.0 0.2 all-reduce.5.cloned.1.call-start
  111.2 65.4 %all-reduce.3.cloned.1.call-done = f32[512,128]{1,0:T(8,128)} async-done(((f32[512,128]{1,0:T(8,128)}), f32[512,128]{1,0:T(8,128)}) %all-reduce.3.cloned.1.call-update) | async-done | bytes 262160 | tf_op jit(solution)/shard_map/psum | solution.py:43
  176.6 0.0 all-reduce.5.cloned.1.call-update
  176.7 149.4 %all-reduce.5.cloned.1.call-done = f32[512,128]{1,0:T(8,128)} async-done(((f32[512,128]{1,0:T(8,128)}), f32[512,128]{1,0:T(8,128)}) %all-reduce.5.cloned.1.call-update) | async-done | bytes 262160 | tf_op jit(solution)/shard_map/psum | solution.py:43
  326.1 1.1 multiply_reduce_fusion.2
  327.2 9.0 %multiply_reduce_fusion = f32[4096]{0:T(1024)S(1)} fusion(f32[4096,128]{0,1:T(8,128)S(1)} %get-tuple-element.10, f32[512,128]{1,0:T(8,128)} %all-reduce.5.cloned.1.call-done, f32[512]{0:T(512)S(1)} %multiply_reduce_fusion.2, f32[4096]{0:T(1024)S(1)} %get-tuple-element.9), kind=kOutput, calls=%fused_computation.18 | convolution fusion | flops 3231707136 | bytes 2394112 | tf_op jit(solution)/shard_map/dot_general | solution.py:46
  336.2 0.0 copy-done.2
  336.2 0.0 copy-done.3
  336.2 0.6 fusion.4
  (5 shorter events, 0.1 us)
Async XLA Ops:
  6.5 80.3 %copy-start = (bf16[1536,128]{1,0:T(8,128)(2,1)S(1)}, bf16[1536,128]{1,0:T(8,128)(2,1)}, u32[]{:S(2)}) copy-start(bf16[1536,128]{1,0:T(8,128)(2,1)} %param.7) | copy-start | bytes 1179652
  6.5 170.1 %all-reduce.3.cloned.1.call-start = ((), (), s32[]{:S(2)}) async-start(), calls=%async_computation | async-start | bytes 524288 | tf_op jit(solution)/shard_map/psum | solution.py:43
  7.8 9.1 %collective-permute-start = (bf16[1,128,1536]{2,1,0:T(8,128)(2,1)S(1)}, bf16[1,128,1536]{2,1,0:T(8,128)(2,1)S(1)}, u32[]{:S(2)}, u32[]{:S(2)}) collective-permute-start(bf16[1,128,1536]{2,1,0:T(8,128)(2,1)S(1)} %get-tuple-element.8), channel_id=1, source_target_pairs={{0,32},{32,64},{64,96},{96,128},{128,160},{160,192},{192,224},{1,3... | collective-permute-start | bytes 1179656 | tf_op jit(solution)/shard_map/ppermute | solution.py:14
  9.7 13.9 %collective-permute-start.1 = (bf16[1,128,1536]{2,1,0:T(8,128)(2,1)S(1)}, bf16[1,128,1536]{2,1,0:T(8,128)(2,1)S(1)}, u32[]{:S(2)}, u32[]{:S(2)}) collective-permute-start(bf16[1,128,1536]{2,1,0:T(8,128)(2,1)S(1)} %get-tuple-element.7), channel_id=1, source_target_pairs={{32,0},{64,32},{96,64},{128,96},{160,128},{192,160},{224,192},{33,... | collective-permute-start | bytes 1179656 | tf_op jit(solution)/shard_map/ppermute | solution.py:17
  23.6 4.8 %copy-start.1 = (bf16[34,128,1536]{2,1,0:T(8,128)(2,1)}, bf16[34,128,1536]{2,1,0:T(8,128)(2,1)S(1)}, u32[]{:S(2)}) copy-start(bf16[34,128,1536]{2,1,0:T(8,128)(2,1)S(1)} %constant_dynamic-update-slice_fusion) | copy-start | bytes 40108036
  28.8 6.3 %collective-permute-start.2 = (bf16[34,1,1536]{2,0,1:T(8,128)(2,1)S(1)}, bf16[34,1,1536]{2,0,1:T(8,128)(2,1)S(1)}, u32[]{:S(2)}, u32[]{:S(2)}) collective-permute-start(bf16[34,1,1536]{2,0,1:T(8,128)(2,1)S(1)} %copy.15), channel_id=1, source_target_pairs={{0,1},{1,2},{2,3},{3,4},{4,5},{5,6},{6,7},{7,8},{8,9},{9,10},{10,1... | collective-permute-start | bytes 313352 | tf_op jit(solution)/shard_map/ppermute | solution.py:14
  32.7 6.8 %collective-permute-start.3 = (bf16[34,1,1536]{2,0,1:T(8,128)(2,1)S(1)}, bf16[34,1,1536]{2,0,1:T(8,128)(2,1)S(1)}, u32[]{:S(2)}, u32[]{:S(2)}) collective-permute-start(bf16[34,1,1536]{2,0,1:T(8,128)(2,1)S(1)} %copy.17), channel_id=1, source_target_pairs={{1,0},{2,1},{3,2},{4,3},{5,4},{6,5},{7,6},{8,7},{9,8},{10,9},{11,1... | collective-permute-start | bytes 313352 | tf_op jit(solution)/shard_map/ppermute | solution.py:17
  105.6 230.6 %copy-start.2 = (f32[32,128]{1,0:T(8,128)S(1)}, f32[32,128]{1,0:T(8,128)}, u32[]{:S(2)}) copy-start(f32[32,128]{1,0:T(8,128)} %param.8) | copy-start | bytes 49156
  105.6 230.6 %copy-start.3 = (s32[32,128]{1,0:T(8,128)S(1)}, s32[32,128]{1,0:T(8,128)}, u32[]{:S(2)}) copy-start(s32[32,128]{1,0:T(8,128)} %param.9) | copy-start | bytes 49156
  111.0 215.1 %all-reduce.5.cloned.1.call-start = ((), (), s32[]{:S(2)}) async-start(), calls=%async_computation.1 | async-start | bytes 524288 | tf_op jit(solution)/shard_map/psum | solution.py:43
Sparse Core Ops, SparseCore 0:
  111.1 65.4 all-reduce.2
  180.5 145.5 all-reduce.4
